TPU v7x, 32 devices: a whole 2x2x4 slice. The times are simulated.
32 devices in a mesh: groups: 2 (over y), tile: 4 (over z), chan: 2 (over x), tm: 2 (over core).
Axes of the slice: x: 2, y: 2, z: 4, core: 2. Of those that a mesh axis runs over, the one named last changes fastest.
Arguments:
- latents: bfloat16 [8, 32, 576], P('tm', 'groups', 'tile'), parts along dimension 1, may hold values from -6 to 6
- tile_order: int32 [8], P('groups'), parts along dimension 0, may hold values from 0 to 3, each once
- w_in: bfloat16 [27, 16, 512], P(None, None, 'chan'), may hold values from -0.3125 to 0.3125
- gain_in: float32 [512], P('chan'), may hold values from 0.25 to 1.75
- shift_in: float32 [512], P('chan'), may hold values from -3 to 3
- w_mid: bfloat16 [27, 512, 512], P(None, None, 'chan'), may hold values from -0.0546875 to 0.0546875
- gain_mid: float32 [512], P('chan'), may hold values from 0.25 to 1.75
- shift_mid: float32 [512], P('chan'), may hold values from -3 to 3
- w_out: bfloat16 [3, 512], P(None, 'chan'), may hold values from -0.25 to 0.25
- blend_weight: float32 [8, 256], P('groups'), parts along dimension 0, may hold values from 0.25 to 4
Outputs:
- decoded: float32 [8, 6, 576], P('tm', 'groups', 'tile'), parts along dimension 1
There are 2 independent parts, one for each index of `groups`. A program takes and returns all parts, laid end to end along the dimension named above; an argument that names none is the same for every part. Nothing has to cross between parts.
Inputs may be any that keep to these rules, and one draw needn't show every extreme that they name: `tile_order`: each image block is held by exactly one latent block.
All inputs are finite; a program needn't handle non-finite values.
Results may differ from a plain program's by a relative error of at most 0.0037.
Values may be sent and summed in bfloat16 or wider, within the bound.
A program may use at most 64 MiB of HBM per device.

v0:
```python
import jax
import jax.numpy as jnp
from jax import lax
from jax.sharding import PartitionSpec as P

CH = 512
GROUPS = 32
TSIDE = 16
STRIDE = 12
GRID_X = 4
EPSILON = 1e-06


def shifted(value, axis, steps):
    count = lax.axis_size(axis)
    leading, last = (max(0, -steps), min(count, count - steps))
    return lax.ppermute(value, axis, [(source, source + steps) for source in range(leading, last)])


def window_index(tile_id, tiles):
    slots = jnp.arange(TSIDE * TSIDE, dtype=jnp.int32)
    row = tile_id // GRID_X * STRIDE + slots // TSIDE
    col = tile_id % GRID_X * STRIDE + slots % TSIDE
    valid = (row < tiles // GRID_X * STRIDE) & (col < GRID_X * STRIDE)
    block = row // STRIDE * GRID_X + col // STRIDE
    index = block * (STRIDE * STRIDE) + row % STRIDE * STRIDE + col % STRIDE
    return (jnp.where(valid, index, 0), valid)


def causal_conv(extended, weights, frames, side):
    pixels = side * side
    rows = jnp.arange(pixels, dtype=jnp.int32) // side
    cols = jnp.arange(pixels, dtype=jnp.int32) % side
    total = jnp.zeros((frames, weights.shape[2], pixels), jnp.float32)
    for depth in range(3):
        window = extended[depth : depth + frames]
        for down in range(3):
            for across in range(3):
                offset = (down - 1) * side + (across - 1)
                inside = (
                    (rows + down - 1 >= 0)
                    & (rows + down - 1 < side)
                    & (cols + across - 1 >= 0)
                    & (cols + across - 1 < side)
                )
                moved = jnp.roll(window, -offset, axis=2)
                moved = jnp.where(inside[None, None, :], moved, jnp.zeros_like(moved))
                total = total + jnp.einsum(
                    "fcp,co->fop",
                    moved,
                    weights[9 * depth + 3 * down + across],
                    preferred_element_type=jnp.float32,
                )
    return total


def with_history(values):
    frames = values.shape[0]
    earlier = shifted(values[frames - 2 :], "tm", 1)
    return jnp.concatenate([earlier, values], axis=0)


def normalize(values, gain, shift, total_frames):
    frames, chans, pixels = values.shape
    width = CH // GROUPS
    grouped = values.reshape(frames, chans // width, width, pixels)
    sums = jnp.sum(grouped, axis=(0, 2, 3))
    squares = jnp.sum(grouped * grouped, axis=(0, 2, 3))
    sums, squares = lax.psum((sums, squares), "tm")
    count = total_frames * width * pixels
    mean = sums / count
    variance = squares / count - mean * mean
    scale = lax.rsqrt(variance + EPSILON)
    normed = (grouped - mean[None, :, None, None]) * scale[None, :, None, None]
    normed = normed.reshape(frames, chans, pixels) * gain[None, :, None] + shift[None, :, None]
    return jax.nn.silu(normed).astype(jnp.bfloat16)


def spread(color, weight, index, total_pixels):
    numer = (
        jnp.zeros((color.shape[0], 3, total_pixels), jnp.float32)
        .at[:, :, index]
        .add(color * weight[None, None, :])
    )
    denom = jnp.zeros((total_pixels,), jnp.float32).at[index].add(weight)
    return (numer, denom)


def route_owned(numer, denom, tile_id, own):
    frames = numer.shape[0]
    margin = (GRID_X + 1) * own
    numer_wide = jnp.concatenate([numer, jnp.zeros((frames, 3, margin), jnp.float32)], axis=2)
    denom_wide = jnp.concatenate([denom, jnp.zeros((margin,), jnp.float32)], axis=0)
    first_pixel = tile_id * own

    def block_at(offset):
        start_pixel = first_pixel + offset * own
        return (
            lax.dynamic_slice_in_dim(numer_wide, start_pixel, own, 2),
            lax.dynamic_slice_in_dim(denom_wide, start_pixel, own, 0),
        )

    owned_numer, owned_denom = block_at(0)
    for offset in (1, GRID_X, GRID_X + 1):
        piece_numer, piece_denom = block_at(offset)
        got_numer, got_denom = shifted((piece_numer, piece_denom), "tile", offset)
        owned_numer = owned_numer + got_numer
        owned_denom = owned_denom + got_denom
    return (owned_numer, owned_denom)


def body(
    latents, tile_order, w_in, gain_in, shift_in, w_mid, gain_mid, shift_mid, w_out, blend_weight
):
    frames = latents.shape[0]
    total_frames = frames * lax.axis_size("tm")
    tiles = tile_order.shape[0]
    own = STRIDE * STRIDE
    total_pixels = tiles * own
    tile_id = lax.axis_index("tile")
    index, valid = window_index(tile_id, tiles)
    whole = lax.all_gather(latents, "tile", axis=2, tiled=True)
    blocks = whole.reshape(frames, whole.shape[1], tiles, own)
    image = (
        jnp.zeros_like(blocks)
        .at[:, :, tile_order]
        .set(blocks)
        .reshape(frames, whole.shape[1], total_pixels)
    )
    window = jnp.where(
        valid[None, None, :], jnp.take(image, index, axis=2), jnp.zeros((), jnp.bfloat16)
    )
    first = causal_conv(with_history(window), w_in, frames, TSIDE)
    hidden = normalize(first, gain_in, shift_in, total_frames)
    second = causal_conv(
        lax.all_gather(with_history(hidden), "chan", axis=1, tiled=True), w_mid, frames, TSIDE
    )
    upper = normalize(second, gain_mid, shift_mid, total_frames)
    color = jnp.einsum("oc,fcp->fop", w_out, upper, preferred_element_type=jnp.float32)
    weight = jnp.where(valid, blend_weight[tile_id], jnp.float32(0.0))
    numer, denom = spread(color, weight, index, total_pixels)
    numer, denom = route_owned(numer, denom, tile_id, own)
    numer = lax.psum(numer, "chan")
    return numer / denom[None, None, :]


def solution(mesh):
    placed = (
        P("tm", "groups", "tile"),
        P("groups"),
        P(None, None, "chan"),
        P("chan"),
        P("chan"),
        P(None, None, "chan"),
        P("chan"),
        P("chan"),
        P(None, "chan"),
        P("groups", None),
    )
    return jax.shard_map(
        body, mesh=mesh, in_specs=placed, out_specs=P("tm", "groups", "tile"), check_vma=False
    )
```

profile of v0, /device:TPU:0, one launch (start us, length us, event | category | flops | bytes accessed | tf_op | source)
XLA Modules:
  0.0 141.7 jit_solution(11770328538480830236)
XLA Ops:
  6.6 1.0 copy.204
  7.6 18.3 %all_gather.6 = bf16[4,16,576]{1,0,2:T(4,128)(2,1)S(1)} all-gather(bf16[4,16,144]{1,0,2:T(4,128)(2,1)S(1)} %copy.204), channel_id=1, replica_groups=mesh['groups'=2,'tile'=4,'chan'=2,'tm'=2] {'tile'}, dimensions={2}, use_global_device_ids=true | all-gather | bytes 92160 | tf_op jit(solution)/shard_map/all_gather | solution.py:122
  26.2 0.7 compare_select_fusion.2
  26.9 0.7 scatter_fusion
  27.9 1.0 gather_fusion
  29.1 1.3 collective-permute-start
  30.5 0.7 collective-permute-done
  31.4 0.4 fusion.206
  33.3 0.4 convolution_add_fusion.13
  36.1 0.4 convolution_add_fusion.6
  36.5 0.4 convolution_add_fusion.5
  36.9 0.4 convolution_add_fusion.4
  39.3 0.4 fusion.8
  39.7 0.4 fusion.7
  40.2 0.4 fusion.6
  42.6 0.4 fusion.503
  43.4 2.5 %all-reduce.3 = (f32[16]{0:T(128)S(1)}, f32[16]{0:T(128)S(1)}) all-reduce(f32[16]{0:T(128)S(1)} %reduce_sum.54, f32[16]{0:T(128)S(1)} %reduce_sum.51), channel_id=1, replica_groups=mesh['groups'=2,'tile'=4,'chan'=2,'tm'=2] {'tm'}, use_global_device_ids=true, to_apply=%region_6.7 | all-reduce | flops 32 | bytes 256 | tf_op jit(solution)/shard_map/psum | solution.py:69
  46.6 2.3 %collective-permute-start.1 = (bf16[2,256,256]{1,2,0:T(8,128)(2,1)S(1)}, bf16[2,256,256]{1,2,0:T(8,128)(2,1)S(1)}, u32[]{:S(2)}, u32[]{:S(2)}) collective-permute-start(bf16[2,256,256]{1,2,0:T(8,128)(2,1)S(1)} %slice.825), channel_id=1, source_target_pairs={{0,1},{2,3},{4,5},{6,7},{8,9},{10,11},{12,13},{14,15},{16,17},{18,... | collective-permute-start | bytes 786440 | tf_op jit(solution)/shard_map/ppermute | solution.py:17
  48.9 1.1 collective-permute-done.1
  50.0 0.9 pad_maximum_fusion
  51.0 2.3 %scatter_custom_fusion.2 = f32[576]{0:T(1024)S(1)} fusion(s32[256]{0:T(256)S(1)} %bitcast.322, f32[256]{0:T(256)S(1)} %broadcast_select_fusion, f32[]{:T(128)} %constant.166.clone.1), kind=kCustom, calls=%fused_computation.579 | custom fusion | flops 256 | bytes 2308 | tf_op jit(solution)/shard_map/scatter-add | solution.py:85
  53.4 3.4 %collective-permute-start.5 = (f32[144]{0:T(256)S(1)}, f32[144]{0:T(256)S(1)}, u32[]{:S(2)}, u32[]{:S(2)}) collective-permute-start(f32[144]{0:T(256)S(1)} %get-tuple-element.115), channel_id=1, source_target_pairs={{0,4},{4,8},{8,12},{1,5},{5,9},{9,13},{2,6},{6,10},{10,14},{3,7},{... | collective-permute-start | bytes 1736 | tf_op jit(solution)/shard_map/ppermute | solution.py:17
  56.9 0.7 collective-permute-start.6
  57.5 0.8 collective-permute-start.7
  58.4 21.1 %all-gather.2.cloned.1.call-done = bf16[6,512,256]{1,2,0:T(8,128)(2,1)} async-done(((bf16[6,256,256]{1,2,0:T(8,128)(2,1)}), bf16[6,512,256]{1,2,0:T(8,128)(2,1)}) %all-gather.2.cloned.1.call-update) | async-done | bytes 1572880 | tf_op jit(solution)/shard_map/all_gather | solution.py:136
  79.5 4.2 %fusion.506 = (bf16[4,512,239]{1,2,0:T(8,128)(2,1)S(1)}, bf16[4,512,239]{1,2,0:T(8,128)(2,1)S(1)}, bf16[4,512,239]{1,2,0:T(8,128)(2,1)S(1)}, bf16[4,512,239]{1,2...) fusion(bf16[6,512,256]{1,2,0:T(8,128)(2,1)} %all-gather.2.cloned.1.call-done), kind=kLoop, calls=%fused_computation.741 | loop fusion | bytes 11747328 | tf_op jit(solution)/shard_map/jit(_roll_static)/slice | solution.py:46
  83.8 1.4 %fusion.23 = f32[4,256,256]{2,1,0:T(8,128)S(1)} fusion(bf16[4,512,239]{1,2,0:T(8,128)(2,1)S(1)} %get-tuple-element.30, bf16[4,512,17]{1,2,0:T(8,128)(2,1)S(1)} %get-tuple-element.36, pred[256]{0:T(512)(128)(4,1)S(1)} %and_and_fusion.8, bf16[27,512,256]{2,1,0:T(8,128)(2,1)} %param.15), kind=kOutput, calls=%fused_computation.84 | convolution fusion | flops 271056896 | bytes 2359552 | tf_op jit(solution)/shard_map/fcp,co->fop/dot_general | solution.py:48
  85.2 1.4 %convolution_bitcast_fusion.8 = f32[4,256,256]{1,2,0:T(8,128)S(1)} fusion(bf16[4,512,239]{1,2,0:T(8,128)(2,1)S(1)} %get-tuple-element.27, bf16[4,512,17]{1,2,0:T(8,128)(2,1)S(1)} %get-tuple-element.33, pred[256]{0:T(512)(128)(4,1)S(1)} %and_and_fusion.8, bf16[27,512,256]{2,1,0:T(8,128)(2,1)} %param.15), kind=kOutput, calls=%fused_computation.12 | convolution fusion | flops 271056896 | bytes 2359552 | tf_op jit(solution)/shard_map/fcp,co->fop/dot_general | solution.py:48
  86.7 0.7 fusion.508
  87.4 1.4 %convolution_bitcast_fusion.7 = f32[4,256,256]{1,2,0:T(8,128)S(1)} fusion(bf16[4,512,240]{1,2,0:T(8,128)(2,1)S(1)} %get-tuple-element.39, bf16[4,512,16]{1,2,0:T(8,128)(2,1)S(1)} %get-tuple-element.45, pred[256]{0:T(512)(128)(4,1)S(1)} %get-tuple-element.131, bf16[27,512,256]{2,1,0:T(8,128)(2,1)} %param.15), kind=kOutput, calls=%fused_computation.11 | convolution fusion | flops 271056896 | bytes 2359552 | tf_op jit(solution)/shard_map/fcp,co->fop/dot_general | solution.py:48
  88.8 0.7 fusion.510
  89.6 1.5 %convolution_bitcast_fusion.6 = f32[4,256,256]{1,2,0:T(8,128)S(1)} fusion(bf16[4,512,241]{1,2,0:T(8,128)(2,1)S(1)} %get-tuple-element.51, bf16[4,512,15]{1,2,0:T(8,128)(2,1)S(1)} %get-tuple-element.57, pred[256]{0:T(512)(128)(4,1)S(1)} %get-tuple-element.130, bf16[27,512,256]{2,1,0:T(8,128)(2,1)} %param.15), kind=kOutput, calls=%fused_computation.10 | convolution fusion | flops 271056896 | bytes 2359552 | tf_op jit(solution)/shard_map/fcp,co->fop/dot_general | solution.py:48
  91.0 0.8 fusion.504
  91.9 1.4 %convolution_bitcast_fusion.5 = f32[4,256,256]{1,2,0:T(8,128)S(1)} fusion(bf16[4,512,255]{1,2,0:T(8,128)(2,1)S(1)} %get-tuple-element.14, bf16[4,512,1]{1,2,0:T(2,128)(2,1)S(1)} %get-tuple-element.20, pred[256]{0:T(512)(128)(4,1)S(1)} %get-tuple-element.129, bf16[27,512,256]{2,1,0:T(8,128)(2,1)} %param.15), kind=kOutput, calls=%fused_computation.9 | convolution fusion | flops 271056896 | bytes 2359552 | tf_op jit(solution)/shard_map/fcp,co->fop/dot_general | solution.py:48
  93.4 1.6 %convolution_bitcast_fusion.2 = f32[4,256,256]{1,2,0:T(8,128)S(1)} fusion(bf16[4,512,15]{1,2,0:T(8,128)(2,1)S(1)} %get-tuple-element.56, bf16[4,512,241]{1,2,0:T(8,128)(2,1)S(1)} %get-tuple-element.50, pred[256]{0:T(512)(128)(4,1)S(1)} %get-tuple-element.126, bf16[27,512,256]{2,1,0:T(8,128)(2,1)} %param.15), kind=kOutput, calls=%fused_computation.6 | convolution fusion | flops 271056896 | bytes 2359552 | tf_op jit(solution)/shard_map/fcp,co->fop/dot_general | solution.py:48
  95.0 1.4 %convolution_bitcast_fusion.1 = f32[4,256,256]{1,2,0:T(8,128)S(1)} fusion(bf16[4,512,16]{1,2,0:T(8,128)(2,1)S(1)} %get-tuple-element.44, bf16[4,512,240]{1,2,0:T(8,128)(2,1)S(1)} %get-tuple-element.38, pred[256]{0:T(512)(128)(4,1)S(1)} %get-tuple-element.125, bf16[27,512,256]{2,1,0:T(8,128)(2,1)} %param.15), kind=kOutput, calls=%fused_computation.5 | convolution fusion | flops 271056896 | bytes 2359552 | tf_op jit(solution)/shard_map/fcp,co->fop/dot_general | solution.py:48
  96.4 1.6 %convolution_bitcast_fusion = f32[4,256,256]{1,2,0:T(8,128)S(1)} fusion(bf16[4,512,17]{1,2,0:T(8,128)(2,1)S(1)} %get-tuple-element.32, bf16[4,512,239]{1,2,0:T(8,128)(2,1)S(1)} %get-tuple-element.26, pred[256]{0:T(512)(128)(4,1)S(1)} %get-tuple-element.124, bf16[27,512,256]{2,1,0:T(8,128)(2,1)} %param.15), kind=kOutput, calls=%fused_computation.4 | convolution fusion | flops 271056896 | bytes 2359552 | tf_op jit(solution)/shard_map/fcp,co->fop/dot_general | solution.py:48
  98.0 1.5 %convolution_add_fusion.31 = f32[4,256,256]{2,1,0:T(8,128)S(1)} fusion(f32[4,256,256]{2,1,0:T(8,128)S(1)} %fusion.23, bf16[4,512,240]{1,2,0:T(8,128)(2,1)S(1)} %get-tuple-element.42, bf16[4,512,16]{1,2,0:T(8,128)(2,1)S(1)} %get-tuple-element.48, pred[256]{0:T(512)(128)(4,1)S(1)} %get-tuple-element.131, bf16[27,512,256]{2,1,0:T(8,128)(2,1)} %param.15), kind=kOutput, calls=%fused_computation.77 | convolution fusion | flops 271319040 | bytes 3408128 | tf_op jit(solution)/shard_map/fcp,co->fop/dot_general | solution.py:48
  99.5 0.5 convolution_add_fusion.30
  100.0 0.5 convolution_add_fusion.29
  100.5 0.5 convolution_add_fusion.28
  101.0 0.5 convolution_add_fusion.27
  101.5 0.5 convolution_add_fusion.26
  102.0 0.5 convolution_add_fusion.25
  102.5 0.5 convolution_add_fusion.24
  103.0 0.5 convolution_add_fusion.23
  103.5 0.5 convolution_add_fusion.22
  104.0 0.5 convolution_add_fusion.21
  104.5 0.5 convolution_add_fusion.20
  105.0 0.5 convolution_add_fusion.19
  105.5 0.5 convolution_add_fusion.18
  106.0 0.7 convolution_add_fusion.17
  106.7 0.5 fusion.21
  107.3 0.5 convolution_bitcast_fusion.4
  107.7 0.6 fusion.16
  108.4 0.6 fusion.502
  109.4 2.5 %all-reduce.2 = (f32[16]{0:T(128)S(1)}, f32[16]{0:T(128)S(1)}) all-reduce(f32[16]{0:T(128)S(1)} %reduce_sum.75, f32[16]{0:T(128)S(1)} %reduce_sum.72), channel_id=1, replica_groups=mesh['groups'=2,'tile'=4,'chan'=2,'tm'=2] {'tm'}, use_global_device_ids=true, to_apply=%region_12.13 | all-reduce | flops 32 | bytes 256 | tf_op jit(solution)/shard_map/psum | solution.py:69
  112.2 0.5 fusion.22
  113.1 8.5 %scatter_fusion.1 = f32[4,3,576]{1,0,2:T(4,128)S(1)} fusion(f32[4,3,576]{1,0,2:T(4,128)S(1)} %broadcast_in_dim.385, s32[256]{0:T(256)S(1)} %bitcast.323, f32[256,4,3]{2,1,0:T(4,128)S(1)} %copy.210), kind=kCustom, calls=%fused_computation.2 | custom fusion | flops 3072 | bytes 37888 | tf_op jit(solution)/shard_map/scatter-add | solution.py:83
  122.2 3.4 %collective-permute-start.2 = (f32[4,3,144]{2,0,1:T(4,128)S(1)}, f32[4,3,144]{2,0,1:T(4,128)S(1)}, u32[]{:S(2)}, u32[]{:S(2)}) collective-permute-start(f32[4,3,144]{2,0,1:T(4,128)S(1)} %get-tuple-element.112), channel_id=1, source_target_pairs={{0,4},{4,8},{8,12},{1,5},{5,9},{9,13},{2,6},{6,10},{10,14},{3,7},{... | collective-permute-start | bytes 20744 | tf_op jit(solution)/shard_map/ppermute | solution.py:17
  125.6 0.7 collective-permute-start.3
  126.2 0.7 collective-permute-start.4
  127.1 7.1 %psum.39 = f32[4,3,144]{2,0,1:T(4,128)S(1)} all-reduce(f32[4,3,144]{2,0,1:T(4,128)S(1)} %fusion.326), channel_id=1, replica_groups=mesh['groups'=2,'tile'=4,'chan'=2,'tm'=2] {'chan'}, use_global_device_ids=true, to_apply=%region_14.15 | all-reduce | flops 1728 | bytes 13824 | tf_op jit(solution)/shard_map/psum | solution.py:143
  134.2 0.6 broadcast_divide_fusion
  (104 shorter events, 11.9 us)
Async XLA Ops:
  6.5 44.4 %copy-start = (f32[4,256]{1,0:T(4,128)S(1)}, f32[4,256]{1,0:T(4,128)}, u32[]{:S(2)}) copy-start(f32[4,256]{1,0:T(4,128)} %param.19) | copy-start | bytes 12292
  6.5 24.9 %copy-start.3 = (bf16[27,16,256]{2,1,0:T(8,128)(2,1)S(1)}, bf16[27,16,256]{2,1,0:T(8,128)(2,1)}, u32[]{:S(2)}) copy-start(bf16[27,16,256]{2,1,0:T(8,128)(2,1)} %param.12) | copy-start | bytes 663556
  6.5 72.9 %all-gather.2.cloned.1.call-start = ((), (), s32[]{:S(2)}) async-start(), calls=%async_computation | async-start | bytes 2359296 | tf_op jit(solution)/shard_map/all_gather | solution.py:136
  29.1 2.1 %collective-permute-start = (bf16[2,16,256]{2,1,0:T(8,128)(2,1)S(1)}, bf16[2,16,256]{2,1,0:T(8,128)(2,1)S(1)}, u32[]{:S(2)}, u32[]{:S(2)}) collective-permute-start(bf16[2,16,256]{2,1,0:T(8,128)(2,1)S(1)} %slice.742), channel_id=1, source_target_pairs={{0,1},{2,3},{4,5},{6,7},{8,9},{10,11},{12,13},{14,15},{16,17},{18,... | collective-permute-start | bytes 49160 | tf_op jit(solution)/shard_map/ppermute | solution.py:17
  42.2 4.1 %copy-start.4 = (f32[256]{0:T(256)S(1)}, f32[256]{0:T(256)}, u32[]{:S(2)}) copy-start(f32[256]{0:T(256)} %param.14) | copy-start | bytes 3076
  42.2 4.0 %copy-start.5 = (f32[256]{0:T(256)S(1)}, f32[256]{0:T(256)}, u32[]{:S(2)}) copy-start(f32[256]{0:T(256)} %param.13) | copy-start | bytes 3076
  46.6 3.4 %collective-permute-start.1 = (bf16[2,256,256]{1,2,0:T(8,128)(2,1)S(1)}, bf16[2,256,256]{1,2,0:T(8,128)(2,1)S(1)}, u32[]{:S(2)}, u32[]{:S(2)}) collective-permute-start(bf16[2,256,256]{1,2,0:T(8,128)(2,1)S(1)} %slice.825), channel_id=1, source_target_pairs={{0,1},{2,3},{4,5},{6,7},{8,9},{10,11},{12,13},{14,15},{16,17},{18,... | collective-permute-start | bytes 786440 | tf_op jit(solution)/shard_map/ppermute | solution.py:17
  53.4 72.8 %collective-permute-start.5 = (f32[144]{0:T(256)S(1)}, f32[144]{0:T(256)S(1)}, u32[]{:S(2)}, u32[]{:S(2)}) collective-permute-start(f32[144]{0:T(256)S(1)} %get-tuple-element.115), channel_id=1, source_target_pairs={{0,4},{4,8},{8,12},{1,5},{5,9},{9,13},{2,6},{6,10},{10,14},{3,7},{... | collective-permute-start | bytes 1736 | tf_op jit(solution)/shard_map/ppermute | solution.py:17
  56.9 70.0 %collective-permute-start.6 = (f32[144]{0:T(256)S(1)}, f32[144]{0:T(256)S(1)}, u32[]{:S(2)}, u32[]{:S(2)}) collective-permute-start(f32[144]{0:T(256)S(1)} %get-tuple-element.116), channel_id=1, source_target_pairs={} | collective-permute-start | bytes 1736 | tf_op jit(solution)/shard_map/ppermute | solution.py:17
  57.5 69.4 %collective-permute-start.7 = (f32[144]{0:T(256)S(1)}, f32[144]{0:T(256)S(1)}, u32[]{:S(2)}, u32[]{:S(2)}) collective-permute-start(f32[144]{0:T(256)S(1)} %get-tuple-element.117), channel_id=1, source_target_pairs={} | collective-permute-start | bytes 1736 | tf_op jit(solution)/shard_map/ppermute | solution.py:17
  79.5 4.2 %copy-start.2 = (bf16[6,512,256]{1,2,0:T(8,128)(2,1)S(1)}, bf16[6,512,256]{1,2,0:T(8,128)(2,1)}, u32[]{:S(2)}) copy-start(bf16[6,512,256]{1,2,0:T(8,128)(2,1)} %all-gather.2.cloned.1.call-done) | copy-start | bytes 4718596
  93.4 6.1 %slice-start = ((s8[7077888]{0:T(1024)(128)(4,1)}), s8[4194304]{0:T(1024)(128)(4,1)S(1)}, s32[]{:S(2)}) async-start(s8[7077888]{0:T(1024)(128)(4,1)} %bitcast.319), calls=%async_computation.1 | async-start | bytes 8388608
  96.4 3.1 %slice-start.1 = ((s8[7077888]{0:T(1024)(128)(4,1)}), s8[2883584]{0:T(1024)(128)(4,1)S(1)}, s32[]{:S(2)}) async-start(s8[7077888]{0:T(1024)(128)(4,1)} %bitcast.319), calls=%async_computation.2 | async-start | bytes 5767168
  108.4 3.8 %copy-start.6 = (bf16[3,256]{1,0:T(4,128)(2,1)S(1)}, bf16[3,256]{1,0:T(4,128)(2,1)}, u32[]{:S(2)}) copy-start(bf16[3,256]{1,0:T(4,128)(2,1)} %param.18) | copy-start | bytes 4612
  108.4 3.8 %copy-start.7 = (f32[256]{0:T(256)S(1)}, f32[256]{0:T(256)}, u32[]{:S(2)}) copy-start(f32[256]{0:T(256)} %param.17) | copy-start | bytes 3076
  108.4 3.8 %copy-start.8 = (f32[256]{0:T(256)S(1)}, f32[256]{0:T(256)}, u32[]{:S(2)}) copy-start(f32[256]{0:T(256)} %param.16) | copy-start | bytes 3076
  112.7 22.2 %copy-start.1 = (f32[4,256]{1,0:T(4,128)S(1)}, f32[4,256]{1,0:T(4,128)}, u32[]{:S(2)}) copy-start(f32[4,256]{1,0:T(4,128)} %param.19) | copy-start | bytes 12292
  122.2 4.8 %collective-permute-start.2 = (f32[4,3,144]{2,0,1:T(4,128)S(1)}, f32[4,3,144]{2,0,1:T(4,128)S(1)}, u32[]{:S(2)}, u32[]{:S(2)}) collective-permute-start(f32[4,3,144]{2,0,1:T(4,128)S(1)} %get-tuple-element.112), channel_id=1, source_target_pairs={{0,4},{4,8},{8,12},{1,5},{5,9},{9,13},{2,6},{6,10},{10,14},{3,7},{... | collective-permute-start | bytes 20744 | tf_op jit(solution)/shard_map/ppermute | solution.py:17
  125.6 1.4 %collective-permute-start.3 = (f32[4,3,144]{2,0,1:T(4,128)S(1)}, f32[4,3,144]{2,0,1:T(4,128)S(1)}, u32[]{:S(2)}, u32[]{:S(2)}) collective-permute-start(f32[4,3,144]{2,0,1:T(4,128)S(1)} %get-tuple-element.113), channel_id=1, source_target_pairs={} | collective-permute-start | bytes 20744 | tf_op jit(solution)/shard_map/ppermute | solution.py:17
  126.2 0.8 collective-permute-start.4
Sparse Core Ops, SparseCore 0:
  51.1 28.3 all-gather.1
where the time goes:
time: 142 us
  matrix products  33.9 us (24%)
  blocking collectives  30.3 us (21%)
  waiting for transfers between devices  23 us (16%)
  other arithmetic  14.9 us (10%)
  between operations  14.3 us (10%)
  starting transfers between devices  13.2 us (9%)
  local copies, waits for them, and re-layouts  12.1 us (9%)
    dot_general x54, matrix products, causal_conv(): jnp.einsum('fcp,co->fop', moved, weights[9 * depth + 3 * down + across],...  33.5 us
    all_gather x1, waiting for transfers between devices, body(): lax.all_gather(with_history(hidden), 'chan', axis=1, tiled=True)  21.1 us
    all_gather x1, blocking collectives, body(): whole = lax.all_gather(latents, 'tile', axis=2, tiled=True)  18.3 us
    ppermute x8, starting transfers between devices, shifted(): lax.ppermute(value, axis, [(source, source + steps) for source in range(l...  13.2 us
    scatter-add x1, other arithmetic, spread(): numer = jnp.zeros((color.shape[0], 3, total_pixels), jnp.float32).at[:, :...  8.52 us
    psum x1, blocking collectives, body(): numer = lax.psum(numer, 'chan')  7.13 us
    slice x8, local copies, waits for them, and re-layouts, causal_conv(): moved = jnp.roll(window, -offset, axis=2)  6.55 us
    psum x2, blocking collectives, normalize(): sums, squares = lax.psum((sums, squares), 'tm')  4.95 us
  transfers between devices with their start and end apart: 9, of which 3 were waited for; matrix products, arithmetic and copies ran while one was open for 30% of the time, Pallas kernels for 0%

commit v1 on v0

--- a/solution.py
+++ b/solution.py
@@ -140,7 +140,7 @@
     weight = jnp.where(valid, blend_weight[tile_id], jnp.float32(0.0))
     numer, denom = spread(color, weight, index, total_pixels)
     numer, denom = route_owned(numer, denom, tile_id, own)
-    numer = lax.psum(numer, "chan")
+    numer = numer + lax.ppermute(numer, "chan", [(0, 1), (1, 0)])
     return numer / denom[None, None, :]
 
 

time: 142 us -> 150 us (1.056)
  waiting for transfers between devices: 23 us -> 36.5 us
  blocking collectives: 30.3 us -> 23.2 us
    ppermute x0 -> x1, waiting for transfers between devices: none -> 7.56 us  [body(): numer = numer + lax.ppermute(numer, 'chan', [(0, 1), (1, 0)])]
    psum x1 -> x0, blocking collectives: 7.13 us -> none  [body(): numer = lax.psum(numer, 'chan')]
    all_gather x1, waiting for transfers between devices: 21.1 us -> 26 us  [body(): lax.all_gather(with_history(hidden), 'chan', axis=1, tiled=True)]
  transfers between devices with their start and end apart: 9 -> 10, of which waited for: 3 -> 5; matrix products, arithmetic and copies ran while one was open for 30% -> 2% of each run, Pallas kernels for 0% -> 0%
where the time goes in v1:
time: 150 us; the launch traced here: 149 us
  waiting for transfers between devices  36.5 us (24%)
  matrix products  33.8 us (23%)
  blocking collectives  23.2 us (15%)
  other arithmetic  14.9 us (10%)
  between operations  14.3 us (10%)
  starting transfers between devices  13.6 us (9%)
  local copies, waits for them, and re-layouts  13.1 us (9%)
    dot_general x54, matrix products, causal_conv(): jnp.einsum('fcp,co->fop', moved, weights[9 * depth + 3 * down + across],...  33.3 us
    all_gather x1, waiting for transfers between devices, body(): lax.all_gather(with_history(hidden), 'chan', axis=1, tiled=True)  26 us
    all_gather x1, blocking collectives, body(): whole = lax.all_gather(latents, 'tile', axis=2, tiled=True)  18.3 us
    ppermute x8, starting transfers between devices, shifted(): lax.ppermute(value, axis, [(source, source + steps) for source in range(l...  13 us
    scatter-add x1, other arithmetic, spread(): numer = jnp.zeros((color.shape[0], 3, total_pixels), jnp.float32).at[:, :...  8.52 us
    ppermute x1, waiting for transfers between devices, body(): numer = numer + lax.ppermute(numer, 'chan', [(0, 1), (1, 0)])  7.56 us
    slice x8, local copies, waits for them, and re-layouts, causal_conv(): moved = jnp.roll(window, -offset, axis=2)  6.65 us
    psum x2, blocking collectives, normalize(): sums, squares = lax.psum((sums, squares), 'tm')  4.95 us
  transfers between devices with their start and end apart: 10, of which 5 were waited for; matrix products, arithmetic and copies ran while one was open for 2% of the time, Pallas kernels for 0%

profile of v1, /device:TPU:0, one launch (start us, length us, event | category | flops | bytes accessed | tf_op | source)
XLA Modules:
  0.0 149.4 jit_solution(7941252291894022096)
XLA Ops:
  6.6 1.0 copy.204
  7.6 18.3 %all_gather.6 = bf16[4,16,576]{1,0,2:T(4,128)(2,1)S(1)} all-gather(bf16[4,16,144]{1,0,2:T(4,128)(2,1)S(1)} %copy.204), channel_id=1, replica_groups=mesh['groups'=2,'tile'=4,'chan'=2,'tm'=2] {'tile'}, dimensions={2}, use_global_device_ids=true | all-gather | bytes 92160 | tf_op jit(solution)/shard_map/all_gather | solution.py:122
  26.2 0.7 compare_select_fusion.2
  26.9 0.7 scatter_fusion
  27.9 1.0 gather_fusion
  29.1 1.3 collective-permute-start
  30.5 0.7 collective-permute-done
  31.4 0.4 fusion.209
  33.3 0.4 convolution_add_fusion.13
  36.9 0.4 convolution_add_fusion.4
  39.3 0.4 fusion.8
  40.2 0.4 fusion.6
  42.6 0.4 fusion.503
  43.4 2.5 %all-reduce.3 = (f32[16]{0:T(128)S(1)}, f32[16]{0:T(128)S(1)}) all-reduce(f32[16]{0:T(128)S(1)} %reduce_sum.54, f32[16]{0:T(128)S(1)} %reduce_sum.51), channel_id=1, replica_groups=mesh['groups'=2,'tile'=4,'chan'=2,'tm'=2] {'tm'}, use_global_device_ids=true, to_apply=%region_6.7 | all-reduce | flops 32 | bytes 256 | tf_op jit(solution)/shard_map/psum | solution.py:69
  46.6 2.3 %collective-permute-start.1 = (bf16[2,256,256]{1,2,0:T(8,128)(2,1)S(1)}, bf16[2,256,256]{1,2,0:T(8,128)(2,1)S(1)}, u32[]{:S(2)}, u32[]{:S(2)}) collective-permute-start(bf16[2,256,256]{1,2,0:T(8,128)(2,1)S(1)} %slice.825), channel_id=1, source_target_pairs={{0,1},{2,3},{4,5},{6,7},{8,9},{10,11},{12,13},{14,15},{16,17},{18,... | collective-permute-start | bytes 786440 | tf_op jit(solution)/shard_map/ppermute | solution.py:17
  48.9 1.1 collective-permute-done.1
  50.0 1.0 pad_maximum_fusion
  51.0 2.5 %scatter_custom_fusion.2 = f32[576]{0:T(1024)S(1)} fusion(s32[256]{0:T(256)S(1)} %bitcast.322, f32[256]{0:T(256)S(1)} %broadcast_select_fusion, f32[]{:T(128)} %constant.166.clone.1), kind=kCustom, calls=%fused_computation.579 | custom fusion | flops 256 | bytes 2308 | tf_op jit(solution)/shard_map/scatter-add | solution.py:85
  53.5 26.0 %all-gather.2.cloned.1.call-done = bf16[6,512,256]{1,2,0:T(8,128)(2,1)} async-done(((bf16[6,256,256]{1,2,0:T(8,128)(2,1)}), bf16[6,512,256]{1,2,0:T(8,128)(2,1)}) %all-gather.2.cloned.1.call-update) | async-done | bytes 1572880 | tf_op jit(solution)/shard_map/all_gather | solution.py:136
  79.5 4.3 %fusion.506 = (bf16[4,512,239]{1,2,0:T(8,128)(2,1)S(1)}, bf16[4,512,239]{1,2,0:T(8,128)(2,1)S(1)}, bf16[4,512,239]{1,2,0:T(8,128)(2,1)S(1)}, bf16[4,512,239]{1,2...) fusion(bf16[6,512,256]{1,2,0:T(8,128)(2,1)} %all-gather.2.cloned.1.call-done), kind=kLoop, calls=%fused_computation.741 | loop fusion | bytes 11747328 | tf_op jit(solution)/shard_map/jit(_roll_static)/slice | solution.py:46
  83.9 1.4 fusion.23
  85.4 1.4 convolution_bitcast_fusion.8
  86.8 0.7 fusion.508
  87.5 1.4 convolution_bitcast_fusion.7
  89.0 0.7 fusion.510
  89.7 1.4 convolution_bitcast_fusion.6
  91.1 0.8 fusion.504
  92.0 1.5 convolution_bitcast_fusion.5
  93.5 1.6 %convolution_bitcast_fusion.2 = f32[4,256,256]{1,2,0:T(8,128)S(1)} fusion(bf16[4,512,15]{1,2,0:T(8,128)(2,1)S(1)} %get-tuple-element.56, bf16[4,512,241]{1,2,0:T(8,128)(2,1)S(1)} %get-tuple-element.50, pred[256]{0:T(512)(128)(4,1)S(1)} %get-tuple-element.126, bf16[27,512,256]{2,1,0:T(8,128)(2,1)} %param.15), kind=kOutput, calls=%fused_computation.10 | convolution fusion | flops 271056896 | bytes 2359552 | tf_op jit(solution)/shard_map/fcp,co->fop/dot_general | solution.py:48
  95.1 1.4 convolution_bitcast_fusion.1
  96.5 1.6 %convolution_bitcast_fusion = f32[4,256,256]{1,2,0:T(8,128)S(1)} fusion(bf16[4,512,17]{1,2,0:T(8,128)(2,1)S(1)} %get-tuple-element.32, bf16[4,512,239]{1,2,0:T(8,128)(2,1)S(1)} %get-tuple-element.26, pred[256]{0:T(512)(128)(4,1)S(1)} %get-tuple-element.124, bf16[27,512,256]{2,1,0:T(8,128)(2,1)} %param.15), kind=kOutput, calls=%fused_computation.8 | convolution fusion | flops 271056896 | bytes 2359552 | tf_op jit(solution)/shard_map/fcp,co->fop/dot_general | solution.py:48
  98.1 1.4 convolution_add_fusion.31
  99.5 0.5 convolution_add_fusion.30
  100.1 0.5 convolution_add_fusion.29
  100.6 0.5 convolution_add_fusion.28
  101.1 0.5 convolution_add_fusion.27
  101.5 0.5 convolution_add_fusion.26
  102.0 0.5 convolution_add_fusion.25
  102.5 0.5 convolution_add_fusion.24
  103.0 0.5 convolution_add_fusion.23
  103.5 0.5 convolution_add_fusion.22
  104.0 0.5 convolution_add_fusion.21
  104.5 0.5 convolution_add_fusion.20
  105.0 0.5 convolution_add_fusion.19
  105.5 0.5 convolution_add_fusion.18
  106.0 0.7 convolution_add_fusion.17
  106.7 0.5 fusion.21
  107.2 0.5 convolution_bitcast_fusion.4
  107.7 0.6 fusion.16
  108.4 0.6 fusion.502
  109.4 2.5 %all-reduce.2 = (f32[16]{0:T(128)S(1)}, f32[16]{0:T(128)S(1)}) all-reduce(f32[16]{0:T(128)S(1)} %reduce_sum.75, f32[16]{0:T(128)S(1)} %reduce_sum.72), channel_id=1, replica_groups=mesh['groups'=2,'tile'=4,'chan'=2,'tm'=2] {'tm'}, use_global_device_ids=true, to_apply=%region_12.13 | all-reduce | flops 32 | bytes 256 | tf_op jit(solution)/shard_map/psum | solution.py:69
  112.2 0.5 fusion.22
  113.1 8.5 %scatter_fusion.1 = f32[4,3,576]{1,0,2:T(4,128)S(1)} fusion(f32[4,3,576]{1,0,2:T(4,128)S(1)} %broadcast_in_dim.385, s32[256]{0:T(256)S(1)} %bitcast.323, f32[256,4,3]{2,1,0:T(4,128)S(1)} %copy.210), kind=kCustom, calls=%fused_computation.2 | custom fusion | flops 3072 | bytes 37888 | tf_op jit(solution)/shard_map/scatter-add | solution.py:83
  121.6 0.7 pad_dynamic-slice_fusion.2
  122.3 3.4 %collective-permute-start.2 = (f32[4,3,144]{1,0,2:T(4,128)S(1)}, f32[4,3,144]{1,0,2:T(4,128)S(1)}, u32[]{:S(2)}, u32[]{:S(2)}) collective-permute-start(f32[4,3,144]{1,0,2:T(4,128)S(1)} %get-tuple-element.61), channel_id=1, source_target_pairs={{0,4},{4,8},{8,12},{1,5},{5,9},{9,13},{2,6},{6,10},{10,14},{3,7},{... | collective-permute-start | bytes 20744 | tf_op jit(solution)/shard_map/ppermute | solution.py:17
  125.7 0.7 collective-permute-start.3
  126.4 0.7 collective-permute-start.4
  127.2 3.4 %collective-permute-start.6 = (f32[144]{0:T(256)S(1)}, f32[144]{0:T(256)S(1)}, u32[]{:S(2)}, u32[]{:S(2)}) collective-permute-start(f32[144]{0:T(256)S(1)} %get-tuple-element.115), channel_id=1, source_target_pairs={{0,4},{4,8},{8,12},{1,5},{5,9},{9,13},{2,6},{6,10},{10,14},{3,7},{... | collective-permute-start | bytes 1736 | tf_op jit(solution)/shard_map/ppermute | solution.py:17
  130.6 0.7 collective-permute-start.7
  131.2 1.1 collective-permute-done.2
  132.3 0.6 collective-permute-start.8
  133.3 0.6 collective-permute-start.5
  134.0 7.6 %collective-permute-done.5 = f32[4,3,144]{1,0,2:T(4,128)S(1)} collective-permute-done((f32[4,3,144]{1,0,2:T(4,128)S(1)}, f32[4,3,144]{1,0,2:T(4,128)S(1)}, u32[]{:S(2)}, u32[]{:S(2)}) %collective-permute-start.5) | collective-permute-done | bytes 6944 | tf_op jit(solution)/shard_map/ppermute | solution.py:143
  141.8 0.8 copy.211
  (105 shorter events, 13.1 us)
Async XLA Ops:
  6.5 44.5 %copy-start = (f32[4,256]{1,0:T(4,128)S(1)}, f32[4,256]{1,0:T(4,128)}, u32[]{:S(2)}) copy-start(f32[4,256]{1,0:T(4,128)} %param.19) | copy-start | bytes 12292
  6.5 24.9 %copy-start.3 = (bf16[27,16,256]{2,1,0:T(8,128)(2,1)S(1)}, bf16[27,16,256]{2,1,0:T(8,128)(2,1)}, u32[]{:S(2)}) copy-start(bf16[27,16,256]{2,1,0:T(8,128)(2,1)} %param.12) | copy-start | bytes 663556
  6.5 73.0 %all-gather.2.cloned.1.call-start = ((), (), s32[]{:S(2)}) async-start(), calls=%async_computation | async-start | bytes 2359296 | tf_op jit(solution)/shard_map/all_gather | solution.py:136
  29.1 2.1 %collective-permute-start = (bf16[2,16,256]{2,1,0:T(8,128)(2,1)S(1)}, bf16[2,16,256]{2,1,0:T(8,128)(2,1)S(1)}, u32[]{:S(2)}, u32[]{:S(2)}) collective-permute-start(bf16[2,16,256]{2,1,0:T(8,128)(2,1)S(1)} %slice.742), channel_id=1, source_target_pairs={{0,1},{2,3},{4,5},{6,7},{8,9},{10,11},{12,13},{14,15},{16,17},{18,... | collective-permute-start | bytes 49160 | tf_op jit(solution)/shard_map/ppermute | solution.py:17
  42.2 4.1 %copy-start.4 = (f32[256]{0:T(256)S(1)}, f32[256]{0:T(256)}, u32[]{:S(2)}) copy-start(f32[256]{0:T(256)} %param.14) | copy-start | bytes 3076
  42.2 4.0 %copy-start.5 = (f32[256]{0:T(256)S(1)}, f32[256]{0:T(256)}, u32[]{:S(2)}) copy-start(f32[256]{0:T(256)} %param.13) | copy-start | bytes 3076
  46.6 3.4 %collective-permute-start.1 = (bf16[2,256,256]{1,2,0:T(8,128)(2,1)S(1)}, bf16[2,256,256]{1,2,0:T(8,128)(2,1)S(1)}, u32[]{:S(2)}, u32[]{:S(2)}) collective-permute-start(bf16[2,256,256]{1,2,0:T(8,128)(2,1)S(1)} %slice.825), channel_id=1, source_target_pairs={{0,1},{2,3},{4,5},{6,7},{8,9},{10,11},{12,13},{14,15},{16,17},{18,... | collective-permute-start | bytes 786440 | tf_op jit(solution)/shard_map/ppermute | solution.py:17
  79.5 4.3 %copy-start.2 = (bf16[6,512,256]{1,2,0:T(8,128)(2,1)S(1)}, bf16[6,512,256]{1,2,0:T(8,128)(2,1)}, u32[]{:S(2)}) copy-start(bf16[6,512,256]{1,2,0:T(8,128)(2,1)} %all-gather.2.cloned.1.call-done) | copy-start | bytes 4718596
  93.5 6.1 %slice-start = ((s8[7077888]{0:T(1024)(128)(4,1)}), s8[4194304]{0:T(1024)(128)(4,1)S(1)}, s32[]{:S(2)}) async-start(s8[7077888]{0:T(1024)(128)(4,1)} %bitcast.319), calls=%async_computation.1 | async-start | bytes 8388608
  96.5 3.0 %slice-start.1 = ((s8[7077888]{0:T(1024)(128)(4,1)}), s8[2883584]{0:T(1024)(128)(4,1)S(1)}, s32[]{:S(2)}) async-start(s8[7077888]{0:T(1024)(128)(4,1)} %bitcast.319), calls=%async_computation.2 | async-start | bytes 5767168
  108.3 3.8 %copy-start.6 = (bf16[3,256]{1,0:T(4,128)(2,1)S(1)}, bf16[3,256]{1,0:T(4,128)(2,1)}, u32[]{:S(2)}) copy-start(bf16[3,256]{1,0:T(4,128)(2,1)} %param.18) | copy-start | bytes 4612
  108.4 3.8 %copy-start.7 = (f32[256]{0:T(256)S(1)}, f32[256]{0:T(256)}, u32[]{:S(2)}) copy-start(f32[256]{0:T(256)} %param.17) | copy-start | bytes 3076
  108.4 3.8 %copy-start.8 = (f32[256]{0:T(256)S(1)}, f32[256]{0:T(256)}, u32[]{:S(2)}) copy-start(f32[256]{0:T(256)} %param.16) | copy-start | bytes 3076
  121.6 21.0 %copy-start.1 = (f32[4,256]{1,0:T(4,128)S(1)}, f32[4,256]{1,0:T(4,128)}, u32[]{:S(2)}) copy-start(f32[4,256]{1,0:T(4,128)} %param.19) | copy-start | bytes 12292
  122.3 10.0 %collective-permute-start.2 = (f32[4,3,144]{1,0,2:T(4,128)S(1)}, f32[4,3,144]{1,0,2:T(4,128)S(1)}, u32[]{:S(2)}, u32[]{:S(2)}) collective-permute-start(f32[4,3,144]{1,0,2:T(4,128)S(1)} %get-tuple-element.61), channel_id=1, source_target_pairs={{0,4},{4,8},{8,12},{1,5},{5,9},{9,13},{2,6},{6,10},{10,14},{3,7},{... | collective-permute-start | bytes 20744 | tf_op jit(solution)/shard_map/ppermute | solution.py:17
  125.7 7.2 %collective-permute-start.3 = (f32[4,3,144]{1,0,2:T(4,128)S(1)}, f32[4,3,144]{1,0,2:T(4,128)S(1)}, u32[]{:S(2)}, u32[]{:S(2)}) collective-permute-start(f32[4,3,144]{1,0,2:T(4,128)S(1)} %get-tuple-element.62), channel_id=1, source_target_pairs={} | collective-permute-start | bytes 20744 | tf_op jit(solution)/shard_map/ppermute | solution.py:17
  126.4 6.6 %collective-permute-start.4 = (f32[4,3,144]{1,0,2:T(4,128)S(1)}, f32[4,3,144]{1,0,2:T(4,128)S(1)}, u32[]{:S(2)}, u32[]{:S(2)}) collective-permute-start(f32[4,3,144]{1,0,2:T(4,128)S(1)} %get-tuple-element.63), channel_id=1, source_target_pairs={} | collective-permute-start | bytes 20744 | tf_op jit(solution)/shard_map/ppermute | solution.py:17
  127.2 6.7 %collective-permute-start.6 = (f32[144]{0:T(256)S(1)}, f32[144]{0:T(256)S(1)}, u32[]{:S(2)}, u32[]{:S(2)}) collective-permute-start(f32[144]{0:T(256)S(1)} %get-tuple-element.115), channel_id=1, source_target_pairs={{0,4},{4,8},{8,12},{1,5},{5,9},{9,13},{2,6},{6,10},{10,14},{3,7},{... | collective-permute-start | bytes 1736 | tf_op jit(solution)/shard_map/ppermute | solution.py:17
  130.6 3.3 %collective-permute-start.7 = (f32[144]{0:T(256)S(1)}, f32[144]{0:T(256)S(1)}, u32[]{:S(2)}, u32[]{:S(2)}) collective-permute-start(f32[144]{0:T(256)S(1)} %get-tuple-element.116), channel_id=1, source_target_pairs={} | collective-permute-start | bytes 1736 | tf_op jit(solution)/shard_map/ppermute | solution.py:17
  132.3 1.6 %collective-permute-start.8 = (f32[144]{0:T(256)S(1)}, f32[144]{0:T(256)S(1)}, u32[]{:S(2)}, u32[]{:S(2)}) collective-permute-start(f32[144]{0:T(256)S(1)} %get-tuple-element.117), channel_id=1, source_target_pairs={} | collective-permute-start | bytes 1736 | tf_op jit(solution)/shard_map/ppermute | solution.py:17
  133.3 8.3 %collective-permute-start.5 = (f32[4,3,144]{1,0,2:T(4,128)S(1)}, f32[4,3,144]{1,0,2:T(4,128)S(1)}, u32[]{:S(2)}, u32[]{:S(2)}) collective-permute-start(f32[4,3,144]{1,0,2:T(4,128)S(1)} %fusion.128), channel_id=1, source_target_pairs={{0,2},{2,0},{1,3},{3,1},{4,6},{6,4},{5,7},{7,5},{8,10},{10,8},{9,1... | collective-permute-start | bytes 20744 | tf_op jit(solution)/shard_map/ppermute | solution.py:143
Sparse Core Ops, SparseCore 0:
  51.1 28.3 all-gather.1
